TPU v7x, 128 devices: a whole 4x4x4 slice. The times are simulated.
128 devices in a mesh: dp: 4 (over y), row: 8 (over z, core), col: 4 (over x).
Axes of the slice: x: 4, y: 4, z: 4, core: 2. Of those that a mesh axis runs over, the one named last changes fastest.
Arguments:
- gradients: bfloat16 [4, 8192, 14336], P('dp', 'row', 'col'), may hold values from -6 to 6
- test_matrix: int32 [14336, 512], P('col'), may hold values from -3 to 3
- old_basis: float32 [8192, 512], P('row'), may hold values from -0.0625 to 0.0625
- first_moment: float32 [512, 14336], P(('dp', 'row'), 'col'), may hold values from -24 to 24
- second_moment: float32 [512, 14336], P(('dp', 'row'), 'col'), may hold values from 1 to 16
Outputs:
- projected: float32 [512, 14336], P(('dp', 'row'), 'col')
- first_moment_new: float32 [512, 14336], P(('dp', 'row'), 'col')
- second_moment_new: float32 [512, 14336], P(('dp', 'row'), 'col')
All inputs are finite; a program needn't handle non-finite values.
Results may differ from a plain program's by a relative error of at most 0.0023.
Values sent between devices are 32-bit elements; how exact they have to be, the bound alone decides.
A program may use at most 128 MiB of HBM per device.

v0:
```python
import jax
import jax.numpy as jnp
from jax import lax
from jax.sharding import PartitionSpec as P

highest = lax.Precision.HIGHEST


def from_partner(value, axis, bit):
    return lax.ppermute(value, axis, [(i, i ^ 1 << bit) for i in range(lax.axis_size(axis))])


def gram_of(row_block):
    return lax.dot_general(
        row_block,
        row_block,
        (((0,), (0,)), ((), ())),
        precision=highest,
        preferred_element_type=jnp.float32,
    )


def basis_from(lower_factor, sketch_part):
    return jax.scipy.linalg.solve_triangular(lower_factor, sketch_part.T, lower=True).T


def local(gradients, test_matrix, old_basis, first_moment, second_moment):
    replica_grad = gradients[0]
    test_values = test_matrix.astype(jnp.bfloat16)
    partial_value = jnp.dot(replica_grad, test_values, preferred_element_type=jnp.float32)
    sketch = lax.psum(partial_value, ("dp", "col"))
    upper_factor = jnp.linalg.cholesky(gram_of(sketch)).T
    for bit_level in range(lax.axis_size("row").bit_length() - 1):
        partner = from_partner(upper_factor, "row", bit_level)
        upper_factor = jnp.linalg.cholesky(gram_of(upper_factor) + gram_of(partner)).T
    new_basis = basis_from(upper_factor.T, sketch)
    basis_low = new_basis.astype(jnp.bfloat16)
    local_correlation = lax.dot_general(
        new_basis,
        old_basis,
        (((0,), (0,)), ((), ())),
        precision=highest,
        preferred_element_type=jnp.float32,
    )
    correlation = lax.psum(local_correlation, "row")
    rank_dev = first_moment.shape[0]
    rank_start = lax.axis_index(("dp", "row")) * rank_dev
    projected = lax.psum_scatter(
        lax.dot_general(
            basis_low, replica_grad, (((0,), (0,)), ((), ())), preferred_element_type=jnp.float32
        ),
        ("dp", "row"),
        scatter_dimension=0,
        tiled=True,
    )
    own_rows = lax.dynamic_slice_in_dim(correlation, rank_start, rank_dev, 0)
    squared = own_rows * own_rows
    turned_first = jnp.dot(
        own_rows,
        lax.all_gather(first_moment, ("dp", "row"), axis=0, tiled=True),
        precision=highest,
        preferred_element_type=jnp.float32,
    )
    turned_second = jnp.dot(
        squared,
        lax.all_gather(second_moment, ("dp", "row"), axis=0, tiled=True),
        precision=highest,
        preferred_element_type=jnp.float32,
    )
    first_new = 0.9 * turned_first + 0.1 * projected
    second_new = 0.95 * turned_second + 0.05 * projected * projected
    return (projected, first_new, second_new)


def solution(mesh):
    in_specs = (
        P("dp", "row", "col"),
        P("col", None),
        P("row", None),
        P(("dp", "row"), "col"),
        P(("dp", "row"), "col"),
    )
    out_specs = (P(("dp", "row"), "col"), P(("dp", "row"), "col"), P(("dp", "row"), "col"))
    return jax.shard_map(local, mesh=mesh, in_specs=in_specs, out_specs=out_specs, check_vma=False)
```

profile of v0, /device:TPU:1, one launch (start us, length us, event | category | flops | bytes accessed | tf_op | source)
XLA Modules:
  0.0 834.7 jit_solution(15446949937610158620)
XLA Ops:
  18.9 92.7 %all-reduce.4.cloned.1.call-done = f32[1024,512]{1,0:T(8,128)} async-done(((f32[1024,512]{1,0:T(8,128)}), f32[1024,512]{1,0:T(8,128)}) %all-reduce.4.cloned.1.call-update) | async-done | bytes 2097168 | tf_op jit(solution)/shard_map/psum | solution.py:31
  121.0 11.7 %cholesky.462 = f32[128,128]{1,0:T(8,128)S(1)} custom-call(f32[128,128]{1,0:T(8,128)S(1)} %cholesky.746), custom_call_target="Cholesky" | custom-call | tf_op jit(solution)/shard_map/jit(cholesky)/cholesky | solution.py:32
  145.2 12.1 %cholesky.481 = f32[128,128]{1,0:T(8,128)S(1)} custom-call(f32[128,128]{1,0:T(8,128)S(1)} %cholesky.750), custom_call_target="Cholesky" | custom-call | tf_op jit(solution)/shard_map/jit(cholesky)/cholesky | solution.py:32
  168.8 11.7 %cholesky.502 = f32[128,128]{1,0:T(8,128)S(1)} custom-call(f32[128,128]{1,0:T(8,128)S(1)} %cholesky.755), custom_call_target="Cholesky" | custom-call | tf_op jit(solution)/shard_map/jit(cholesky)/cholesky | solution.py:32
  192.4 11.9 %cholesky.519 = f32[128,128]{1,0:T(8,128)S(1)} custom-call(f32[128,128]{1,0:T(8,128)S(1)} %convolution_subtract_fusion.4), custom_call_target="Cholesky" | custom-call | tf_op jit(solution)/shard_map/jit(cholesky)/cholesky | solution.py:32
  218.3 11.7 %cholesky.534 = f32[128,128]{1,0:T(8,128)S(1)} custom-call(f32[128,128]{1,0:T(8,128)S(1)} %cholesky.759), custom_call_target="Cholesky" | custom-call | tf_op jit(solution)/shard_map/jit(cholesky)/cholesky | solution.py:35
  242.5 12.1 %cholesky.553 = f32[128,128]{1,0:T(8,128)S(1)} custom-call(f32[128,128]{1,0:T(8,128)S(1)} %cholesky.763), custom_call_target="Cholesky" | custom-call | tf_op jit(solution)/shard_map/jit(cholesky)/cholesky | solution.py:35
  267.3 11.7 %cholesky.574 = f32[128,128]{1,0:T(8,128)S(1)} custom-call(f32[128,128]{1,0:T(8,128)S(1)} %cholesky.768), custom_call_target="Cholesky" | custom-call | tf_op jit(solution)/shard_map/jit(cholesky)/cholesky | solution.py:35
  291.1 11.7 %cholesky.591 = f32[128,128]{1,0:T(8,128)S(1)} custom-call(f32[128,128]{1,0:T(8,128)S(1)} %slice_subtract_fusion.8), custom_call_target="Cholesky" | custom-call | tf_op jit(solution)/shard_map/jit(cholesky)/cholesky | solution.py:35
  309.5 21.2 %collective-permute-done.1 = f32[512,512]{0,1:T(8,128)S(1)} collective-permute-done((f32[512,512]{0,1:T(8,128)S(1)}, f32[512,512]{0,1:T(8,128)S(1)}, u32[]{:S(2)}, u32[]{:S(2)}) %collective-permute-start.1) | collective-permute-done | bytes 1048608 | tf_op jit(solution)/shard_map/ppermute | solution.py:10
  336.3 11.7 %cholesky.606 = f32[128,128]{1,0:T(8,128)S(1)} custom-call(f32[128,128]{1,0:T(8,128)S(1)} %cholesky.772), custom_call_target="Cholesky" | custom-call | tf_op jit(solution)/shard_map/jit(cholesky)/cholesky | solution.py:35
  360.5 12.1 %cholesky.625 = f32[128,128]{1,0:T(8,128)S(1)} custom-call(f32[128,128]{1,0:T(8,128)S(1)} %cholesky.776), custom_call_target="Cholesky" | custom-call | tf_op jit(solution)/shard_map/jit(cholesky)/cholesky | solution.py:35
  385.3 11.7 %cholesky.646 = f32[128,128]{1,0:T(8,128)S(1)} custom-call(f32[128,128]{1,0:T(8,128)S(1)} %cholesky.781), custom_call_target="Cholesky" | custom-call | tf_op jit(solution)/shard_map/jit(cholesky)/cholesky | solution.py:35
  409.1 11.7 %cholesky.663 = f32[128,128]{1,0:T(8,128)S(1)} custom-call(f32[128,128]{1,0:T(8,128)S(1)} %slice_subtract_fusion.7), custom_call_target="Cholesky" | custom-call | tf_op jit(solution)/shard_map/jit(cholesky)/cholesky | solution.py:35
  430.0 20.5 %collective-permute-done.2 = f32[512,512]{0,1:T(8,128)} collective-permute-done((f32[512,512]{0,1:T(8,128)}, f32[512,512]{0,1:T(8,128)}, u32[]{:S(2)}, u32[]{:S(2)}) %collective-permute-start.2) | collective-permute-done | bytes 1048608 | tf_op jit(solution)/shard_map/ppermute | solution.py:10
  457.7 11.7 %cholesky.678 = f32[128,128]{1,0:T(8,128)S(1)} custom-call(f32[128,128]{1,0:T(8,128)S(1)} %cholesky.785), custom_call_target="Cholesky" | custom-call | tf_op jit(solution)/shard_map/jit(cholesky)/cholesky | solution.py:35
  481.9 12.1 %cholesky.697 = f32[128,128]{1,0:T(8,128)S(1)} custom-call(f32[128,128]{1,0:T(8,128)S(1)} %cholesky.789), custom_call_target="Cholesky" | custom-call | tf_op jit(solution)/shard_map/jit(cholesky)/cholesky | solution.py:35
  506.7 11.7 %cholesky.718 = f32[128,128]{1,0:T(8,128)S(1)} custom-call(f32[128,128]{1,0:T(8,128)S(1)} %cholesky.794), custom_call_target="Cholesky" | custom-call | tf_op jit(solution)/shard_map/jit(cholesky)/cholesky | solution.py:35
  530.5 11.7 %cholesky.735 = f32[128,128]{1,0:T(8,128)S(1)} custom-call(f32[128,128]{1,0:T(8,128)S(1)} %slice_subtract_fusion.6), custom_call_target="Cholesky" | custom-call | tf_op jit(solution)/shard_map/jit(cholesky)/cholesky | solution.py:35
  546.4 14.0 %while.1 = (s32[]{:T(128)}, f32[512,512]{1,0:T(8,128)}, s32[4,2]{0,1:T(2,128)S(1)}, f32[4,128,128]{2,1,0:T(8,128)}, s32[]{:T(128)}) while((s32[]{:T(128)}, f32[512,512]{1,0:T(8,128)}, s32[4,2]{0,1:T(2,128)S(1)}, f32[4,128,128]{2,1,0:T(8,128)}, s32[]{:T(128)}) %tuple.53), condition=%wide.while_cond, body=%wide.while_body.sunk | while | flops 2 | bytes 132705 | solution.py:24
  560.4 40.1 %custom-call.24 = f32[4,128,128]{1,2,0:T(8,128)S(1)} custom-call(f32[4,128,128]{2,1,0:T(8,128)} %get-tuple-element.11), custom_call_target="InvertDiagBlocksLowerTriangular" | custom-call | tf_op jit(solution)/shard_map/jit(_solve_triangular)/triangular_solve | solution.py:24
  630.1 55.8 %all-reduce.6.cloned.1.call-done = f32[512,512]{1,0:T(8,128)} async-done(((f32[512,512]{1,0:T(8,128)}), f32[512,512]{1,0:T(8,128)}) %all-reduce.6.cloned.1.call-update) | async-done | bytes 1048592 | tf_op jit(solution)/shard_map/psum | solution.py:45
  685.9 79.3 %reduce-scatter.2.cloned.1.call-done = f32[16,3584]{1,0:T(8,128)} async-done(((f32[512,3584]{1,0:T(8,128)}), f32[16,3584]{1,0:T(8,128)}) %reduce-scatter.2.cloned.1.call-update) | async-done | bytes 229392 | tf_op jit(solution)/shard_map/reduce_scatter | solution.py:48
  772.5 47.0 %all-gather.3.cloned.1.call-done = f32[512,3584]{1,0:T(8,128)} async-done(((f32[16,3584]{1,0:T(8,128)}), f32[512,3584]{1,0:T(8,128)}) %all-gather.3.cloned.1.call-update) | async-done | bytes 7340048 | tf_op jit(solution)/shard_map/all_gather | solution.py:60
  (162 shorter events, 262.4 us)
Async XLA Ops:
  8.0 605.8 %copy-start = (f32[1024,512]{1,0:T(8,128)S(1)}, f32[1024,512]{1,0:T(8,128)}, u32[]{:S(2)}) copy-start(f32[1024,512]{1,0:T(8,128)} %param.8) | copy-start | bytes 6291460
  8.0 103.5 %all-reduce.4.cloned.1.call-start = ((), (), s32[]{:S(2)}) async-start(), calls=%async_computation.1 | async-start | bytes 4194304 | tf_op jit(solution)/shard_map/psum | solution.py:31
  18.6 667.3 %all-reduce.6.cloned.1.call-start = ((), (), s32[]{:S(2)}) async-start(), calls=%async_computation.3 | async-start | bytes 2097152 | tf_op jit(solution)/shard_map/psum | solution.py:45
  120.0 1.0 copy-start.6
  208.3 4.4 collective-permute-start
  217.3 1.0 copy-start.4
  306.2 24.4 %collective-permute-start.1 = (f32[512,512]{0,1:T(8,128)S(1)}, f32[512,512]{0,1:T(8,128)S(1)}, u32[]{:S(2)}, u32[]{:S(2)}) collective-permute-start(f32[512,512]{0,1:T(8,128)S(1)} %fusion.28), channel_id=1, source_target_pairs={{0,8},{4,12},{8,0},{12,4},{16,24},{20,28},{24,16},{28,20},{1,9},{5... | collective-permute-start | bytes 3145736 | tf_op jit(solution)/shard_map/ppermute | solution.py:10
  335.3 1.0 copy-start.5
  425.2 25.3 %collective-permute-start.2 = (f32[512,512]{0,1:T(8,128)}, f32[512,512]{0,1:T(8,128)}, u32[]{:S(2)}, u32[]{:S(2)}) collective-permute-start(f32[512,512]{0,1:T(8,128)} %fusion.30), channel_id=1, source_target_pairs={{0,16},{4,20},{8,24},{12,28},{16,0},{20,4},{24,8},{28,12},{1,17},{... | collective-permute-start | bytes 3145736 | tf_op jit(solution)/shard_map/ppermute | solution.py:10
  456.7 1.0 copy-start.3
  600.5 4.6 copy-start.1
  608.5 4.5 copy-start.2
  613.0 0.8 copy-start.7
  618.4 67.5 %all-gather.5.cloned.1.call-start = ((), (), s32[]{:S(2)}) async-start(), calls=%async_computation.5 | async-start | bytes 7569408 | tf_op jit(solution)/shard_map/all_gather | solution.py:66
  618.9 146.2 %reduce-scatter.2.cloned.1.call-start = ((), (), s32[]{:S(2)}) async-start(), calls=%async_computation.2 | async-start | bytes 7569408 | tf_op jit(solution)/shard_map/reduce_scatter | solution.py:48
  629.6 190.0 %all-gather.3.cloned.1.call-start = ((), (), s32[]{:S(2)}) async-start(), calls=%async_computation.4 | async-start | bytes 7569408 | tf_op jit(solution)/shard_map/all_gather | solution.py:60
  765.2 54.4 %copy-start.8 = (f32[16,3584]{1,0:T(8,128)S(1)}, f32[16,3584]{1,0:T(8,128)}, u32[]{:S(2)}) copy-start(f32[16,3584]{1,0:T(8,128)} %reduce-scatter.2.cloned.1.call-done) | copy-start | bytes 688132
Sparse Core Ops, SparseCore 0:
  18.8 92.7 all-reduce.3
  618.5 67.3 all-reduce.5
Sparse Core Ops, SparseCore 1:
  621.1 53.5 all-gather.4
  678.9 86.3 reduce-scatter.1
  767.3 52.2 all-gather.2
where the time goes:
time: 838 us; the launch traced here: 835 us
  other arithmetic  365 us (44%)
  waiting for transfers between devices  318 us (38%)
  matrix products  93.3 us (11%)
  between operations  26.7 us (3%)
  local copies, waits for them, and re-layouts  24.6 us (3%)
    another operation x45, other arithmetic, local(): jnp.linalg.cholesky(gram_of(upper_factor) + gram_of(partner))  238 us
    psum x1, waiting for transfers between devices, local(): sketch = lax.psum(partial_value, ('dp', 'col'))  92.7 us
    reduce_scatter x1, waiting for transfers between devices, local(): lax.psum_scatter(lax.dot_general(basis_low, replica_grad, (((0,), (0,)),...  79.3 us
    another operation x14, other arithmetic, local(): upper_factor = jnp.linalg.cholesky(gram_of(sketch)).T  78.9 us
    psum x1, waiting for transfers between devices, local(): correlation = lax.psum(local_correlation, 'row')  55.8 us
    all_gather x1, waiting for transfers between devices, local(): lax.all_gather(first_moment, ('dp', 'row'), axis=0, tiled=True)  47 us
    ppermute x3, waiting for transfers between devices, from_partner(): lax.ppermute(value, axis, [(i, i ^ 1 << bit) for i in range(lax.axis_size...  42.1 us
    another operation x3, other arithmetic, basis_from(): jax.scipy.linalg.solve_triangular(lower_factor, sketch_part.T, lower=True)  41.2 us
  transfers between devices with their start and end apart: 8, of which 7 were waited for; matrix products, arithmetic and copies ran while one was open for 3% of the time, Pallas kernels for 0%

commit v1 on v0

--- a/solution.py
+++ b/solution.py
@@ -42,7 +42,7 @@
         precision=highest,
         preferred_element_type=jnp.float32,
     )
-    correlation = lax.psum(local_correlation, "row")
+    correlation = jnp.sum(lax.all_gather(local_correlation, "row"), axis=0)
     rank_dev = first_moment.shape[0]
     rank_start = lax.axis_index(("dp", "row")) * rank_dev
     projected = lax.psum_scatter(

time: 838 us -> 883 us (1.054)
  waiting for transfers between devices: 318 us -> 361 us
    psum x1 -> x0, waiting for transfers between devices: 55.8 us -> none  [local(): correlation = lax.psum(local_correlation, 'row')]
    all_gather x1, waiting for transfers between devices: 0.01 us -> 48.7 us  [local(): lax.all_gather(second_moment, ('dp', 'row'), axis=0, tiled=True)]
    all_gather x0 -> x1, waiting for transfers between devices: none -> 39.4 us  [local(): correlation = jnp.sum(lax.all_gather(local_correlation, 'row'), axis=0)]
    reduce_scatter x1, waiting for transfers between devices: 79.3 us -> 89.8 us  [local(): lax.psum_scatter(lax.dot_general(basis_low, replica_grad, (((0,), (0,)),...]
  transfers between devices with their start and end apart: 8 -> 8, of which waited for: 7 -> 8; matrix products, arithmetic and copies ran while one was open for 3% -> 3% of each run, Pallas kernels for 0% -> 0%
where the time goes in v1:
time: 883 us; the launch traced here: 879 us
  other arithmetic  370 us (42%)
  waiting for transfers between devices  361 us (41%)
  matrix products  92.4 us (10%)
  between operations  24.8 us (3%)
  local copies, waits for them, and re-layouts  24.6 us (3%)
    another operation x45, other arithmetic, local(): jnp.linalg.cholesky(gram_of(upper_factor) + gram_of(partner))  238 us
    psum x1, waiting for transfers between devices, local(): sketch = lax.psum(partial_value, ('dp', 'col'))  92.7 us
    reduce_scatter x1, waiting for transfers between devices, local(): lax.psum_scatter(lax.dot_general(basis_low, replica_grad, (((0,), (0,)),...  89.8 us
    another operation x14, other arithmetic, local(): upper_factor = jnp.linalg.cholesky(gram_of(sketch)).T  78.9 us
    all_gather x1, waiting for transfers between devices, local(): lax.all_gather(second_moment, ('dp', 'row'), axis=0, tiled=True)  48.7 us
    all_gather x1, waiting for transfers between devices, local(): lax.all_gather(first_moment, ('dp', 'row'), axis=0, tiled=True)  47 us
    ppermute x3, waiting for transfers between devices, from_partner(): lax.ppermute(value, axis, [(i, i ^ 1 << bit) for i in range(lax.axis_size...  42.1 us
    another operation x3, other arithmetic, basis_from(): jax.scipy.linalg.solve_triangular(lower_factor, sketch_part.T, lower=True)  41.2 us
  transfers between devices with their start and end apart: 8, of which 8 were waited for; matrix products, arithmetic and copies ran while one was open for 3% of the time, Pallas kernels for 0%

profile of v1, /device:TPU:1, one launch (start us, length us, event | category | flops | bytes accessed | tf_op | source)
XLA Modules:
  0.0 879.5 jit_solution(4543384066974148495)
XLA Ops:
  18.0 92.7 %all-reduce.3.cloned.1.call-done = f32[1024,512]{1,0:T(8,128)} async-done(((f32[1024,512]{1,0:T(8,128)}), f32[1024,512]{1,0:T(8,128)}) %all-reduce.3.cloned.1.call-update) | async-done | bytes 2097168 | tf_op jit(solution)/shard_map/psum | solution.py:31
  120.2 11.7 %cholesky.462 = f32[128,128]{1,0:T(8,128)S(1)} custom-call(f32[128,128]{1,0:T(8,128)S(1)} %cholesky.746), custom_call_target="Cholesky" | custom-call | tf_op jit(solution)/shard_map/jit(cholesky)/cholesky | solution.py:32
  144.4 12.1 %cholesky.481 = f32[128,128]{1,0:T(8,128)S(1)} custom-call(f32[128,128]{1,0:T(8,128)S(1)} %cholesky.750), custom_call_target="Cholesky" | custom-call | tf_op jit(solution)/shard_map/jit(cholesky)/cholesky | solution.py:32
  167.9 11.7 %cholesky.502 = f32[128,128]{1,0:T(8,128)S(1)} custom-call(f32[128,128]{1,0:T(8,128)S(1)} %cholesky.755), custom_call_target="Cholesky" | custom-call | tf_op jit(solution)/shard_map/jit(cholesky)/cholesky | solution.py:32
  191.6 11.9 %cholesky.519 = f32[128,128]{1,0:T(8,128)S(1)} custom-call(f32[128,128]{1,0:T(8,128)S(1)} %convolution_subtract_fusion.4), custom_call_target="Cholesky" | custom-call | tf_op jit(solution)/shard_map/jit(cholesky)/cholesky | solution.py:32
  217.5 11.7 %cholesky.534 = f32[128,128]{1,0:T(8,128)S(1)} custom-call(f32[128,128]{1,0:T(8,128)S(1)} %cholesky.759), custom_call_target="Cholesky" | custom-call | tf_op jit(solution)/shard_map/jit(cholesky)/cholesky | solution.py:35
  241.7 12.1 %cholesky.553 = f32[128,128]{1,0:T(8,128)S(1)} custom-call(f32[128,128]{1,0:T(8,128)S(1)} %cholesky.763), custom_call_target="Cholesky" | custom-call | tf_op jit(solution)/shard_map/jit(cholesky)/cholesky | solution.py:35
  266.5 11.7 %cholesky.574 = f32[128,128]{1,0:T(8,128)S(1)} custom-call(f32[128,128]{1,0:T(8,128)S(1)} %cholesky.768), custom_call_target="Cholesky" | custom-call | tf_op jit(solution)/shard_map/jit(cholesky)/cholesky | solution.py:35
  290.3 11.7 %cholesky.591 = f32[128,128]{1,0:T(8,128)S(1)} custom-call(f32[128,128]{1,0:T(8,128)S(1)} %slice_subtract_fusion.8), custom_call_target="Cholesky" | custom-call | tf_op jit(solution)/shard_map/jit(cholesky)/cholesky | solution.py:35
  308.6 21.2 %collective-permute-done.1 = f32[512,512]{0,1:T(8,128)S(1)} collective-permute-done((f32[512,512]{0,1:T(8,128)S(1)}, f32[512,512]{0,1:T(8,128)S(1)}, u32[]{:S(2)}, u32[]{:S(2)}) %collective-permute-start.1) | collective-permute-done | bytes 1048608 | tf_op jit(solution)/shard_map/ppermute | solution.py:10
  335.5 11.7 %cholesky.606 = f32[128,128]{1,0:T(8,128)S(1)} custom-call(f32[128,128]{1,0:T(8,128)S(1)} %cholesky.772), custom_call_target="Cholesky" | custom-call | tf_op jit(solution)/shard_map/jit(cholesky)/cholesky | solution.py:35
  359.7 12.1 %cholesky.625 = f32[128,128]{1,0:T(8,128)S(1)} custom-call(f32[128,128]{1,0:T(8,128)S(1)} %cholesky.776), custom_call_target="Cholesky" | custom-call | tf_op jit(solution)/shard_map/jit(cholesky)/cholesky | solution.py:35
  384.5 11.7 %cholesky.646 = f32[128,128]{1,0:T(8,128)S(1)} custom-call(f32[128,128]{1,0:T(8,128)S(1)} %cholesky.781), custom_call_target="Cholesky" | custom-call | tf_op jit(solution)/shard_map/jit(cholesky)/cholesky | solution.py:35
  408.3 11.7 %cholesky.663 = f32[128,128]{1,0:T(8,128)S(1)} custom-call(f32[128,128]{1,0:T(8,128)S(1)} %slice_subtract_fusion.7), custom_call_target="Cholesky" | custom-call | tf_op jit(solution)/shard_map/jit(cholesky)/cholesky | solution.py:35
  429.1 20.5 %collective-permute-done.2 = f32[512,512]{0,1:T(8,128)} collective-permute-done((f32[512,512]{0,1:T(8,128)}, f32[512,512]{0,1:T(8,128)}, u32[]{:S(2)}, u32[]{:S(2)}) %collective-permute-start.2) | collective-permute-done | bytes 1048608 | tf_op jit(solution)/shard_map/ppermute | solution.py:10
  456.8 11.7 %cholesky.678 = f32[128,128]{1,0:T(8,128)S(1)} custom-call(f32[128,128]{1,0:T(8,128)S(1)} %cholesky.785), custom_call_target="Cholesky" | custom-call | tf_op jit(solution)/shard_map/jit(cholesky)/cholesky | solution.py:35
  481.0 12.1 %cholesky.697 = f32[128,128]{1,0:T(8,128)S(1)} custom-call(f32[128,128]{1,0:T(8,128)S(1)} %cholesky.789), custom_call_target="Cholesky" | custom-call | tf_op jit(solution)/shard_map/jit(cholesky)/cholesky | solution.py:35
  505.8 11.7 %cholesky.718 = f32[128,128]{1,0:T(8,128)S(1)} custom-call(f32[128,128]{1,0:T(8,128)S(1)} %cholesky.794), custom_call_target="Cholesky" | custom-call | tf_op jit(solution)/shard_map/jit(cholesky)/cholesky | solution.py:35
  545.6 14.0 %while.1 = (s32[]{:T(128)}, f32[512,512]{1,0:T(8,128)}, s32[4,2]{0,1:T(2,128)S(1)}, f32[4,128,128]{2,1,0:T(8,128)}, s32[]{:T(128)}) while((s32[]{:T(128)}, f32[512,512]{1,0:T(8,128)}, s32[4,2]{0,1:T(2,128)S(1)}, f32[4,128,128]{2,1,0:T(8,128)}, s32[]{:T(128)}) %tuple.53), condition=%wide.while_cond, body=%wide.while_body.sunk | while | flops 2 | bytes 132705 | solution.py:24
  559.6 40.1 %custom-call.24 = f32[4,128,128]{1,2,0:T(8,128)S(1)} custom-call(f32[4,128,128]{2,1,0:T(8,128)} %get-tuple-element.11), custom_call_target="InvertDiagBlocksLowerTriangular" | custom-call | tf_op jit(solution)/shard_map/jit(_solve_triangular)/triangular_solve | solution.py:24
  629.6 39.4 %all-gather.9.cloned.1.call-done = f32[4096,512]{1,0:T(8,128)} async-done(((f32[512,512]{1,0:T(8,128)}), f32[4096,512]{1,0:T(8,128)}) %all-gather.9.cloned.1.call-update) | async-done | bytes 8388624 | tf_op jit(solution)/shard_map/all_gather | solution.py:45
  673.4 48.7 %all-gather.7.cloned.1.call-done = f32[512,3584]{1,0:T(8,128)} async-done(((f32[16,3584]{1,0:T(8,128)}), f32[512,3584]{1,0:T(8,128)}) %all-gather.7.cloned.1.call-update) | async-done | bytes 7340048 | tf_op jit(solution)/shard_map/all_gather | solution.py:66
  722.2 89.8 %reduce-scatter.2.cloned.1.call-done = f32[16,3584]{1,0:T(8,128)} async-done(((f32[512,3584]{1,0:T(8,128)}), f32[16,3584]{1,0:T(8,128)}) %reduce-scatter.2.cloned.1.call-update) | async-done | bytes 229392 | tf_op jit(solution)/shard_map/reduce_scatter | solution.py:48
  819.4 47.0 %all-gather.5.cloned.1.call-done = f32[512,3584]{1,0:T(8,128)} async-done(((f32[16,3584]{1,0:T(8,128)}), f32[512,3584]{1,0:T(8,128)}) %all-gather.5.cloned.1.call-update) | async-done | bytes 7340048 | tf_op jit(solution)/shard_map/all_gather | solution.py:60
  (163 shorter events, 278.0 us)
Async XLA Ops:
  7.2 605.8 %copy-start = (f32[1024,512]{1,0:T(8,128)S(1)}, f32[1024,512]{1,0:T(8,128)}, u32[]{:S(2)}) copy-start(f32[1024,512]{1,0:T(8,128)} %param.8) | copy-start | bytes 6291460
  7.2 103.5 %all-reduce.3.cloned.1.call-start = ((), (), s32[]{:S(2)}) async-start(), calls=%async_computation.1 | async-start | bytes 4194304 | tf_op jit(solution)/shard_map/psum | solution.py:31
  17.8 651.1 %all-gather.9.cloned.1.call-start = ((), (), s32[]{:S(2)}) async-start(), calls=%async_computation.5 | async-start | bytes 9437184 | tf_op jit(solution)/shard_map/all_gather | solution.py:45
  119.2 1.0 copy-start.6
  207.5 4.4 collective-permute-start
  216.5 1.0 copy-start.3
  305.4 24.4 %collective-permute-start.1 = (f32[512,512]{0,1:T(8,128)S(1)}, f32[512,512]{0,1:T(8,128)S(1)}, u32[]{:S(2)}, u32[]{:S(2)}) collective-permute-start(f32[512,512]{0,1:T(8,128)S(1)} %fusion.28), channel_id=1, source_target_pairs={{0,8},{4,12},{8,0},{12,4},{16,24},{20,28},{24,16},{28,20},{1,9},{5... | collective-permute-start | bytes 3145736 | tf_op jit(solution)/shard_map/ppermute | solution.py:10
  334.5 1.0 copy-start.4
  424.4 25.3 %collective-permute-start.2 = (f32[512,512]{0,1:T(8,128)}, f32[512,512]{0,1:T(8,128)}, u32[]{:S(2)}, u32[]{:S(2)}) collective-permute-start(f32[512,512]{0,1:T(8,128)} %fusion.30), channel_id=1, source_target_pairs={{0,16},{4,20},{8,24},{12,28},{16,0},{20,4},{24,8},{28,12},{1,17},{... | collective-permute-start | bytes 3145736 | tf_op jit(solution)/shard_map/ppermute | solution.py:10
  455.8 1.0 copy-start.5
  599.7 4.6 copy-start.1
  607.7 4.5 copy-start.2
  612.2 0.8 copy-start.7
  617.5 104.7 %all-gather.7.cloned.1.call-start = ((), (), s32[]{:S(2)}) async-start(), calls=%async_computation.4 | async-start | bytes 7569408 | tf_op jit(solution)/shard_map/all_gather | solution.py:66
  618.2 193.7 %reduce-scatter.2.cloned.1.call-start = ((), (), s32[]{:S(2)}) async-start(), calls=%async_computation.2 | async-start | bytes 7569408 | tf_op jit(solution)/shard_map/reduce_scatter | solution.py:48
  629.0 237.3 %all-gather.5.cloned.1.call-start = ((), (), s32[]{:S(2)}) async-start(), calls=%async_computation.3 | async-start | bytes 7569408 | tf_op jit(solution)/shard_map/all_gather | solution.py:60
  812.0 54.3 %copy-start.8 = (f32[16,3584]{1,0:T(8,128)S(1)}, f32[16,3584]{1,0:T(8,128)}, u32[]{:S(2)}) copy-start(f32[16,3584]{1,0:T(8,128)} %reduce-scatter.2.cloned.1.call-done) | copy-start | bytes 688132
Sparse Core Ops, SparseCore 0:
  17.9 92.7 all-reduce.2
  617.6 51.2 all-gather.8
  671.2 50.9 all-gather.6
  726.4 85.5 reduce-scatter.1
  814.1 52.1 all-gather.4
